TPU v7x, 128 devices: a whole 4x4x4 slice. The times are simulated.
128 devices in a mesh: req: 4 (over z), blk: 32 (over y, x, core).
Axes of the slice: x: 4, y: 4, z: 4, core: 2. Of those that a mesh axis runs over, the one named last changes fastest.
Arguments:
- tree_input: bfloat16 [6144, 1280], P(('req', 'blk')), may hold values from -6 to 6
- cache: bfloat16 [4, 2, 65536, 1280], P('req', None, 'blk'), may hold values from -1200 to 1200, as said below
- page_table: int32 [4, 512], P('req'), may hold values from 0 to 511, each once within a row
- lengths: int32 [4, 32], P('req'), may hold values from 1 to 32768, 57344 in all within a row
- parents: int32 [128, 48], P(('req', 'blk')), may hold values from 0 to 29, as said below
- accept_leaf: int32 [4, 32], P('req'), may hold values from 0 to 47
- w_qkv: bfloat16 [1280, 3840], P(None, 'blk'), may hold values from -0.15625 to 0.15625
- w_out: bfloat16 [1280, 1280], P(None, 'blk'), may hold values from -0.15625 to 0.15625
- w_up: bfloat16 [1280, 1280], P(None, 'blk'), may hold values from -0.15625 to 0.15625
- w_down: bfloat16 [1280, 1280], P('blk'), may hold values from -0.15625 to 0.15625
- w_draft: bfloat16 [4, 1280, 1280], P(None, None, 'blk'), may hold values from -0.15625 to 0.15625
- w_patch: bfloat16 [1280, 1280], P(None, 'req'), may hold values from -0.15625 to 0.15625
Outputs:
- layer_out: bfloat16 [6144, 1280], P(('req', 'blk'))
- drafts: bfloat16 [4, 6144, 1280], P(None, ('req', 'blk'))
- cache_new: bfloat16 [4, 2, 65536, 1280], P('req', None, 'blk')
Inputs may be any that keep to these rules, and one draw needn't show every extreme that they name: `cache`: keys of the pool may hold a few rows of far larger size. `parents`: node 0 is its own parent. The nodes form 5 levels of sizes 1, 4, 10, 15, 18 in index order, and every other node's parent lies in the level before its own. `page_table`: row g holds the pool pages of group g; request r's pages are the npages_r entries after those of requests before it (see the steps), and page p is held by index p // 16 of blk.
All inputs are finite; a program needn't handle non-finite values.
Results may differ from a plain program's by a relative error of at most 0.018.
The roundings to bfloat16 on the way count: a program that leaves them out, or rounds other values in their place, can miss the bound.
Values may be sent and summed in bfloat16 or wider, within the bound.
A program may use at most 192 MiB of HBM per device.

v0:
```python
import math
import jax
import jax.numpy as jnp
from jax import lax
from jax.sharding import PartitionSpec as P

H = 16
HD = 80
TREE = 48
DEPTH = 5
PAGE = 128
EPS = 1e-06
NEG = -1e30
LEVEL_START = (0, 1, 5, 15, 30, 48)


def rms_rows(values):
    wide = values.astype(jnp.float32)
    return (wide * lax.rsqrt(jnp.mean(wide * wide, axis=-1, keepdims=True) + EPS)).astype(
        jnp.bfloat16
    )


def ancestors(parent_rows):
    nodes = jnp.arange(TREE, dtype=jnp.int32)
    current = jnp.broadcast_to(nodes, parent_rows.shape)
    marks = current[:, :, None] == nodes[None, None, :]
    for level in range(DEPTH - 1):
        current = jnp.take_along_axis(parent_rows, current, axis=1)
        marks = marks | (current[:, :, None] == nodes[None, None, :])
    return marks


def row_blocks(values, mapper):
    return mapper(lax.all_gather(values, "blk", axis=0, tiled=True), jnp.int32(0))


def column_blocks(values):
    return lax.all_to_all(values, "blk", split_axis=0, concat_axis=1, tiled=True)


def on_device(
    tree_input,
    cache,
    page_table,
    lengths,
    parents,
    accept_leaf,
    w_qkv,
    w_out,
    w_up,
    w_down,
    w_draft,
    w_patch,
):
    blocks = lax.axis_size("blk")
    myself = lax.axis_index("blk")
    tree_rows = tree_input.shape[0]
    width = tree_input.shape[1]
    requests = lengths.shape[1]
    pool_pages = cache.shape[2] // PAGE
    scale = 1.0 / math.sqrt(HD)
    normed = rms_rows(tree_input)

    def project_qkv(piece, start):
        return jnp.dot(piece, w_qkv, preferred_element_type=jnp.float32).astype(jnp.bfloat16)

    projected_part = row_blocks(normed, project_qkv)
    projected = column_blocks(projected_part)
    key_own = projected[:, width : 2 * width]
    value_own = projected[:, 2 * width :]
    query_all = lax.all_gather(projected[:, :width], "blk", axis=0, tiled=True)
    page_row = page_table[0]
    length_row = lengths[0]
    leaf_row = accept_leaf[0]
    total_pages = page_row.shape[0]
    npages = (length_row + DEPTH + PAGE - 1) // PAGE
    page_ends = jnp.cumsum(npages)
    offsets = page_ends - npages
    local_ids = myself * pool_pages + jnp.arange(pool_pages, dtype=jnp.int32)
    located = page_row[None, :] == local_ids[:, None]
    where_at = jnp.sum(
        jnp.where(located, jnp.arange(total_pages, dtype=jnp.int32)[None, :], 0), axis=1
    )
    owner = jnp.sum((page_ends[None, :] <= where_at[:, None]).astype(jnp.int32), axis=1)
    owner_hot = owner[:, None] == jnp.arange(requests, dtype=jnp.int32)[None, :]
    safe_owner = jnp.minimum(owner, requests - 1)
    page_len = jnp.sum(jnp.where(owner_hot, length_row[None, :], 0), axis=1)
    page_offset = jnp.sum(jnp.where(owner_hot, offsets[None, :], 0), axis=1)
    positions = (where_at - page_offset)[:, None] * PAGE + jnp.arange(PAGE, dtype=jnp.int32)[
        None, :
    ]
    valid = positions < page_len[:, None]
    query4 = query_all.reshape(requests, tree_rows, H, HD)
    query_page = jnp.take(query4, safe_owner, axis=0)
    keys = cache[0, 0].reshape(pool_pages, PAGE, H, HD)
    values = cache[0, 1].reshape(pool_pages, PAGE, H, HD)
    scores = (
        jnp.einsum("pqhd,pthd->pqht", query_page, keys, preferred_element_type=jnp.float32) * scale
    )
    masked = jnp.where(valid[:, None, None, :], scores, NEG)
    page_max = jnp.max(masked, axis=-1)
    request_max = jnp.max(jnp.where(owner_hot.T[:, :, None, None], page_max[None], NEG), axis=1)
    page_top = jnp.take(request_max, safe_owner, axis=0)
    weights = jnp.where(valid[:, None, None, :], jnp.exp(masked - page_top[..., None]), 0.0)
    page_den = jnp.sum(weights, axis=-1)
    page_num = jnp.einsum(
        "pqht,pthd->pqhd", weights.astype(jnp.bfloat16), values, preferred_element_type=jnp.float32
    )
    hot = owner_hot.astype(jnp.float32)
    den_part = jnp.einsum("pr,pqh->rqh", hot, page_den, precision=lax.Precision.HIGHEST)
    num_part = jnp.einsum("pr,pqhd->rqhd", hot, page_num, precision=lax.Precision.HIGHEST).reshape(
        requests, tree_rows, width
    )
    max_all = lax.pmax(request_max, "blk")
    factor = jnp.exp(request_max - max_all)
    den_scaled = den_part * factor
    num_scaled = (num_part.reshape(requests, tree_rows, H, HD) * factor[..., None]).reshape(
        requests, tree_rows, width
    )
    den_own, num_own = (
        lax.psum_scatter(den_scaled, "blk", scatter_dimension=0, tiled=True),
        lax.psum_scatter(num_scaled, "blk", scatter_dimension=0, tiled=True),
    )
    cache_top = lax.dynamic_slice_in_dim(max_all, myself, 1, 0)[0]
    cache_den = den_own[0]
    cache_num = num_own[0]
    marks = ancestors(parents)[0]
    query_own = lax.dynamic_slice_in_dim(query_all, myself * tree_rows, tree_rows, 0).reshape(
        tree_rows, H, HD
    )
    key_tree = key_own.reshape(tree_rows, H, HD)
    value_tree = value_own.reshape(tree_rows, H, HD)
    tree_scores = (
        jnp.einsum("qhd,khd->qhk", query_own, key_tree, preferred_element_type=jnp.float32) * scale
    )
    tree_masked = jnp.where(marks[:, None, :], tree_scores, NEG)
    row_top = jnp.maximum(cache_top, jnp.max(tree_masked, axis=-1))
    tree_weights = jnp.where(marks[:, None, :], jnp.exp(tree_masked - row_top[..., None]), 0.0)
    carried = jnp.exp(cache_top - row_top)
    denom = cache_den * carried + jnp.sum(tree_weights, axis=-1)
    numer = cache_num.reshape(tree_rows, H, HD) * carried[..., None] + jnp.einsum(
        "qhk,khd->qhd",
        tree_weights.astype(jnp.bfloat16),
        value_tree,
        preferred_element_type=jnp.float32,
    )
    attended = (numer / denom[..., None]).reshape(tree_rows, width).astype(jnp.bfloat16)

    def project_out(piece, start):
        return jnp.dot(piece, w_out, preferred_element_type=jnp.float32).astype(jnp.bfloat16)

    proj = column_blocks(row_blocks(attended, project_out))
    mid = (tree_input.astype(jnp.float32) + proj.astype(jnp.float32)).astype(jnp.bfloat16)

    def project_up(piece, start):
        return jax.nn.gelu(jnp.dot(piece, w_up, preferred_element_type=jnp.float32)).astype(
            jnp.bfloat16
        )

    hidden_all = row_blocks(rms_rows(mid), project_up)
    feedforward = lax.psum_scatter(
        jnp.dot(hidden_all, w_down, preferred_element_type=jnp.float32),
        "blk",
        scatter_dimension=0,
        tiled=True,
    )
    layer_out = (mid.astype(jnp.float32) + feedforward).astype(jnp.bfloat16)
    head_count = w_draft.shape[0]
    head_cols = w_draft.shape[2]

    def project_draft(piece, start):
        grown = jnp.einsum("nd,kdc->nkc", piece, w_draft, preferred_element_type=jnp.float32)
        return (
            jax.nn.silu(grown).astype(jnp.bfloat16).reshape(piece.shape[0], head_count * head_cols)
        )

    branch = column_blocks(row_blocks(rms_rows(layer_out), project_draft))
    branch = (
        branch.reshape(tree_rows, blocks, head_count, head_cols)
        .transpose(2, 0, 1, 3)
        .reshape(head_count, tree_rows, width)
    )
    drafted = (layer_out.astype(jnp.float32)[None] + branch.astype(jnp.float32)).astype(
        jnp.bfloat16
    )
    drafts = jnp.einsum(
        "krd,do->kro",
        drafted,
        lax.all_gather(w_patch, "req", axis=1, tiled=True),
        preferred_element_type=jnp.float32,
    ).astype(jnp.bfloat16)
    my_leaf = lax.dynamic_slice_in_dim(leaf_row, myself, 1, 0)
    chosen = jnp.take(marks, my_leaf, axis=0)[0]
    ranks = jnp.cumsum(chosen.astype(jnp.int32)) - 1
    picker = chosen[None, :] & (ranks[None, :] == jnp.arange(DEPTH, dtype=jnp.int32)[:, None])
    both_rows = jnp.concatenate([key_own, value_own], axis=1)
    send_rows = jnp.dot(
        picker.astype(jnp.bfloat16), both_rows, preferred_element_type=jnp.float32
    ).astype(jnp.bfloat16)
    received = lax.all_gather(send_rows, "blk", axis=0, tiled=True)
    level_marks = jnp.asarray(LEVEL_START[1:-1], jnp.int32)
    accepted_count = 1 + jnp.sum(
        (leaf_row[:, None] >= level_marks[None, :]).astype(jnp.int32), axis=1
    )
    steps_ahead = jnp.arange(DEPTH, dtype=jnp.int32)
    written = length_row[:, None] + steps_ahead[None, :]
    page_index = jnp.take(
        page_row, jnp.clip(offsets[:, None] + written // PAGE, 0, total_pages - 1)
    )
    keeper = (steps_ahead[None, :] < accepted_count[:, None]) & (page_index // pool_pages == myself)
    target = jnp.where(
        keeper, page_index % pool_pages * PAGE + written % PAGE, pool_pages * PAGE
    ).reshape(-1)
    new_keys = cache[0, 0].at[target].set(received[:, :width], mode="drop")
    new_values = cache[0, 1].at[target].set(received[:, width:], mode="drop")
    cache_new = jnp.stack([new_keys, new_values])[None]
    return (layer_out, drafts, cache_new)


def solution(mesh):
    in_specs = (
        P(("req", "blk"), None),
        P("req", None, "blk", None),
        P("req", None),
        P("req", None),
        P(("req", "blk"), None),
        P("req", None),
        P(None, "blk"),
        P(None, "blk"),
        P(None, "blk"),
        P("blk", None),
        P(None, None, "blk"),
        P(None, "req"),
    )
    out_specs = (
        P(("req", "blk"), None),
        P(None, ("req", "blk"), None),
        P("req", None, "blk", None),
    )
    return jax.shard_map(
        on_device, mesh=mesh, in_specs=in_specs, out_specs=out_specs, check_vma=False
    )
```

profile of v0, /device:TPU:1, one launch (start us, length us, event | category | flops | bytes accessed | tf_op | source)
XLA Modules:
  0.0 739.8 jit_solution(1722064064987440074)
XLA Ops:
  10.0 50.1 %all-gather.8.cloned.1.call-done = bf16[1536,1280]{1,0:T(8,128)(2,1)} async-done(((bf16[48,1280]{1,0:T(8,128)(2,1)}), bf16[1536,1280]{1,0:T(8,128)(2,1)}) %all-gather.8.cloned.1.call-update) | async-done | bytes 3932176 | tf_op jit(solution)/shard_map/all_gather | solution.py:35
  60.1 3.5 convolution_convert_fusion.1
  63.9 15.2 %all_to_all.45 = bf16[32,48,120]{2,1,0:T(8,128)(2,1)S(1)} all-to-all(bf16[32,48,120]{2,1,0:T(8,128)(2,1)S(1)} %bitcast.182), channel_id=1, replica_groups=mesh['req'=4,'blk'=32] {'blk'}, dimensions={0} | all-to-all | bytes 737280 | tf_op jit(solution)/shard_map/all_to_all | solution.py:39
  81.0 10.6 %slice_bitcast_fusion.1 = (bf16[2048,1280]{1,0:T(8,128)(2,1)}, bf16[2048,1280]{1,0:T(8,128)(2,1)}, bf16[1,1,2048,1280]{3,2,1,0:T(8,128)(2,1)}, bf16[1,1,2048,1280]{3,2,1,0:T(8,128)(2,1)}) fusion(bf16[1,2,2048,1280]{3,2,1,0:T(8,128)(2,1)} %param.16), kind=kLoop, calls=%fused_computation.218 | loop fusion | bytes 31457280 | tf_op jit(solution)/shard_map/squeeze | solution.py:215
  91.6 15.7 %reshape.1047 = bf16[16,128,16,80]{3,2,1,0:T(8,128)(2,1)} reshape(bf16[1,1,2048,1280]{3,2,1,0:T(8,128)(2,1)} %get-tuple-element.30) | data formatting | bytes 10485760 | tf_op jit(solution)/shard_map/reshape;squeeze | solution.py:96
  107.3 15.8 %reshape.1048 = bf16[16,128,16,80]{3,2,1,0:T(8,128)(2,1)} reshape(bf16[1,1,2048,1280]{3,2,1,0:T(8,128)(2,1)} %get-tuple-element.29) | data formatting | bytes 10485760 | tf_op jit(solution)/shard_map/reshape;squeeze | solution.py:97
  124.2 12.1 %reshape.896 = bf16[32,48,16,80]{3,2,1,0:T(8,128)(2,1)} reshape(bf16[1536,1280]{1,0:T(8,128)(2,1)} %all-gather.10.cloned.1.call-done) | data formatting | bytes 7864320 | tf_op jit(solution)/shard_map/reshape | solution.py:94
  136.2 5.4 gather_fusion
  143.9 10.6 %bitcast_reduce_fusion = (f32[16,48,16]{1,2,0:T(8,128)S(1)}, f32[16,16,48,128]{3,2,1,0:T(8,128)}) fusion(pred[16,128]{1,0:T(8,128)(4,1)S(1)} %add_compare_fusion, bf16[16,128,16,80]{3,2,1,0:T(8,128)(2,1)} %reshape.1047, bf16[16,48,16,80]{3,2,1,0:T(8,128)(2,1)S(1)} %broadcast_select_fusion), kind=kOutput, calls=%fused_computation.15 | convolution fusion | flops 256364544 | bytes 13551616 | tf_op jit(solution)/shard_map/pqhd,pthd->pqht/dot_general | solution.py:99
  157.2 9.4 %fusion.23 = f32[16,48,16,80]{3,1,2,0:T(8,128)} fusion(bf16[16,128,16,80]{3,2,1,0:T(8,128)(2,1)} %reshape.1048, f32[16,16,48,128]{3,2,1,0:T(8,128)} %get-tuple-element.38, f32[16,48,16]{1,2,0:T(8,128)S(1)} %broadcast_select_fusion.1, pred[16,128]{1,0:T(8,128)(4,1)S(1)} %add_compare_fusion), kind=kOutput, calls=%fused_computation.37 | convolution fusion | flops 259522560 | bytes 15517696 | tf_op jit(solution)/shard_map/pqht,pthd->pqhd/dot_general | solution.py:107
  166.6 3.7 fusion.8
  170.3 86.9 %all-reduce.2.cloned.1.call-done = f32[32,48,16]{1,0,2:T(8,128)} async-done(((f32[32,48,16]{1,0,2:T(8,128)}), f32[32,48,16]{1,0,2:T(8,128)}) %all-reduce.2.cloned.1.call-update) | async-done | bytes 98320 | tf_op jit(solution)/shard_map/pmax | solution.py:115
  259.9 13.2 %broadcast_multiply_fusion = f32[32,48,16,80]{3,0,2,1:T(8,128)} fusion(f32[32,48,16]{0,2,1:T(8,128)S(1)} %copy.110, f32[16,48,16,80]{3,1,2,0:T(8,128)} %fusion.23, s32[16]{0:T(128)S(1)} %convert_reduce_fusion), kind=kOutput, calls=%fused_computation.20 | convolution fusion | flops 379453952 | bytes 11894848 | tf_op jit(solution)/shard_map/pr,pqhd->rqhd/dot_general | solution.py:112
  273.0 16.4 %copy.111 = f32[32,48,16,80]{3,2,1,0:T(8,128)} copy(f32[32,48,16,80]{3,0,2,1:T(8,128)} %broadcast_multiply_fusion) | data formatting | bytes 15728640 | tf_op jit(solution)/shard_map/mul | solution.py:118
  289.5 12.8 %reshape.897 = f32[32,48,1280]{2,1,0:T(8,128)} reshape(f32[32,48,16,80]{3,2,1,0:T(8,128)} %copy.111) | data formatting | bytes 15728640 | tf_op jit(solution)/shard_map/reshape | solution.py:118
  309.3 26.3 %reduce-scatter.6.cloned.1.call-done = f32[1,48,16]{1,2,0:T(8,128)} async-done(((f32[32,48,16]{1,2,0:T(8,128)}), f32[1,48,16]{1,2,0:T(8,128)}) %reduce-scatter.6.cloned.1.call-update) | async-done | bytes 3088 | tf_op jit(solution)/shard_map/reduce_scatter | solution.py:122
  336.4 93.1 %reduce-scatter.4.cloned.1.call-done = f32[1,48,1280]{2,1,0:T(8,128)} async-done(((f32[32,48,1280]{2,1,0:T(8,128)}), f32[1,48,1280]{2,1,0:T(8,128)}) %reduce-scatter.4.cloned.1.call-update) | async-done | bytes 245776 | tf_op jit(solution)/shard_map/reduce_scatter | solution.py:123
  432.1 47.4 %all-gather.12.cloned.1.call-done = bf16[1536,1280]{1,0:T(8,128)(2,1)} async-done(((bf16[48,1280]{1,0:T(8,128)(2,1)}), bf16[1536,1280]{1,0:T(8,128)(2,1)}) %all-gather.12.cloned.1.call-update) | async-done | bytes 3932176 | tf_op jit(solution)/shard_map/all_gather | solution.py:35
  479.5 3.4 convolution_convert_fusion.2
  483.8 12.7 %all_to_all.46 = bf16[32,2,960]{2,1,0:T(2,128)(2,1)S(1)} all-to-all(bf16[32,2,960]{2,1,0:T(2,128)(2,1)S(1)} %reshape.1056), channel_id=1, replica_groups=mesh['req'=4,'blk'=32] {'blk'}, dimensions={0} | all-to-all | bytes 245760 | tf_op jit(solution)/shard_map/all_to_all | solution.py:39
  498.2 43.7 %all-gather.14.cloned.1.call-done = bf16[1536,1280]{1,0:T(8,128)(2,1)} async-done(((bf16[48,1280]{1,0:T(8,128)(2,1)}), bf16[1536,1280]{1,0:T(8,128)(2,1)}) %all-gather.14.cloned.1.call-update) | async-done | bytes 3932176 | tf_op jit(solution)/shard_map/all_gather | solution.py:35
  541.9 7.8 %fusion.66 = f32[1536,1280]{1,0:T(8,128)} fusion(bf16[40,1280]{1,0:T(8,128)(2,1)S(1)} %copy-done.7, bf16[1536,1280]{1,0:T(8,128)(2,1)} %all-gather.14.cloned.1.call-done, bf16[1280,40]{0,1:T(8,128)(2,1)S(1)} %copy-done.8), kind=kOutput, calls=%fused_computation.93 | convolution fusion | flops 315125760 | bytes 12001280 | tf_op jit(solution)/shard_map/dot_general | solution.py:163
  549.8 87.3 %reduce-scatter.8.cloned.1.call-done = f32[48,1280]{1,0:T(8,128)} async-done(((f32[1536,1280]{1,0:T(8,128)}), f32[48,1280]{1,0:T(8,128)}) %reduce-scatter.8.cloned.1.call-update) | async-done | bytes 245776 | tf_op jit(solution)/shard_map/reduce_scatter | solution.py:162
  645.3 26.9 %all-gather = bf16[32,5,2560]{2,1,0:T(8,128)(2,1)S(1)} all-gather(bf16[1,5,2560]{2,1,0:T(8,128)(2,1)S(1)} %fusion.12), channel_id=1, replica_groups=mesh['req'=4,'blk'=32] {'blk'}, dimensions={0}, use_global_device_ids=true | all-gather | bytes 844800 | tf_op jit(solution)/shard_map/all_gather | solution.py:201
  672.6 7.1 scatter_custom_fusion
  679.7 7.3 scatter_custom_fusion.1
  687.4 3.5 fusion.119
  694.5 5.6 all-to-all-start.2
  700.1 9.1 %maximum_bitcast_fusion = bf16[1,2,2048,1280]{3,2,1,0:T(8,128)(2,1)} fusion(bf16[1,2048,1280]{2,1,0:T(8,128)(2,1)} %bitcast.177, bf16[1,2048,1280]{2,1,0:T(8,128)(2,1)} %bitcast.178), kind=kLoop, calls=%fused_computation.9 | loop fusion | flops 5242880 | bytes 20971520 | tf_op jit(solution)/shard_map/broadcast_in_dim | solution.py:217
  709.2 5.1 all-to-all-done.2
  718.2 4.1 copy.125
  728.8 3.9 fusion.28
  (156 shorter events, 47.2 us)
Async XLA Ops:
  7.2 680.3 %copy-start = (bf16[4,1280,40]{1,2,0:T(8,128)(2,1)S(1)}, bf16[4,1280,40]{1,2,0:T(8,128)(2,1)}, u32[]{:S(2)}) copy-start(bf16[4,1280,40]{1,2,0:T(8,128)(2,1)} %param.25) | copy-start | bytes 1228804
  7.2 53.0 %all-gather.8.cloned.1.call-start = ((), (), s32[]{:S(2)}) async-start(), calls=%async_computation.6 | async-start | bytes 4055040 | tf_op jit(solution)/shard_map/all_gather | solution.py:35
  8.3 72.4 %copy-start.9 = (s32[1,32]{1,0:T(1,128)S(1)}, s32[1,32]{1,0:T(1,128)}, u32[]{:S(2)}) copy-start(s32[1,32]{1,0:T(1,128)} %param.18) | copy-start | bytes 388
  10.0 114.2 %all-gather.10.cloned.1.call-start = ((), (), s32[]{:S(2)}) async-start(), calls=%async_computation.7 | async-start | bytes 4055040 | tf_op jit(solution)/shard_map/all_gather | solution.py:72
  80.5 176.7 %all-reduce.2.cloned.1.call-start = ((), (), s32[]{:S(2)}) async-start(), calls=%async_computation.8 | async-start | bytes 524288 | tf_op jit(solution)/shard_map/pmax | solution.py:115
  107.3 15.8 %copy-start.1 = (s32[1,512]{1,0:T(1,128)S(1)}, s32[1,512]{1,0:T(1,128)}, u32[]{:S(2)}) copy-start(s32[1,512]{1,0:T(1,128)} %param.17) | copy-start | bytes 6148
  156.8 9.8 %slice-start = ((s8[6291456]{0:T(1024)(128)(4,1)}), s8[2097152]{0:T(1024)(128)(4,1)S(1)}, s32[]{:S(2)}) async-start(s8[6291456]{0:T(1024)(128)(4,1)} %bitcast.175), calls=%async_computation.16 | async-start | bytes 4194304
  156.9 178.8 %reduce-scatter.6.cloned.1.call-start = ((), (), s32[]{:S(2)}) async-start(), calls=%async_computation.10 | async-start | bytes 270336 | tf_op jit(solution)/shard_map/reduce_scatter | solution.py:122
  157.2 9.5 %slice-start.1 = ((s8[6291456]{0:T(1024)(128)(4,1)}), s8[4194304]{0:T(1024)(128)(4,1)S(1)}, s32[]{:S(2)}) async-start(s8[6291456]{0:T(1024)(128)(4,1)} %bitcast.175), calls=%async_computation.17 | async-start | bytes 8388608
  259.8 169.7 %reduce-scatter.4.cloned.1.call-start = ((), (), s32[]{:S(2)}) async-start(), calls=%async_computation.9 | async-start | bytes 8110080 | tf_op jit(solution)/shard_map/reduce_scatter | solution.py:123
  302.3 0.7 copy-start.2
  302.3 4.0 copy-start.5
  302.3 177.3 %copy-start.6 = (bf16[1280,40]{0,1:T(8,128)(2,1)S(1)}, bf16[1280,40]{0,1:T(8,128)(2,1)}, u32[]{:S(2)}) copy-start(bf16[1280,40]{0,1:T(8,128)(2,1)} %param.22) | copy-start | bytes 307204
  302.3 177.2 %all-gather.12.cloned.1.call-start = ((), (), s32[]{:S(2)}) async-start(), calls=%async_computation.11 | async-start | bytes 4055040 | tf_op jit(solution)/shard_map/all_gather | solution.py:35
  431.1 66.1 %copy-start.3 = (bf16[48,1280]{1,0:T(8,128)(2,1)S(1)}, bf16[48,1280]{1,0:T(8,128)(2,1)}, u32[]{:S(2)}) copy-start(bf16[48,1280]{1,0:T(8,128)(2,1)} %param.15) | copy-start | bytes 368644
  432.0 109.9 %copy-start.7 = (bf16[40,1280]{1,0:T(8,128)(2,1)S(1)}, bf16[40,1280]{1,0:T(8,128)(2,1)}, u32[]{:S(2)}) copy-start(bf16[40,1280]{1,0:T(8,128)(2,1)} %param.24) | copy-start | bytes 307204
  432.1 109.9 %copy-start.8 = (bf16[1280,40]{0,1:T(8,128)(2,1)S(1)}, bf16[1280,40]{0,1:T(8,128)(2,1)}, u32[]{:S(2)}) copy-start(bf16[1280,40]{0,1:T(8,128)(2,1)} %param.23) | copy-start | bytes 307204
  432.1 109.8 %all-gather.14.cloned.1.call-start = ((), (), s32[]{:S(2)}) async-start(), calls=%async_computation.12 | async-start | bytes 4055040 | tf_op jit(solution)/shard_map/all_gather | solution.py:35
  498.1 138.9 %reduce-scatter.8.cloned.1.call-start = ((), (), s32[]{:S(2)}) async-start(), calls=%async_computation.13 | async-start | bytes 8110080 | tf_op jit(solution)/shard_map/reduce_scatter | solution.py:162
  549.7 89.8 %copy-start.10 = (s32[1,32]{1,0:T(1,128)S(1)}, s32[1,32]{1,0:T(1,128)}, u32[]{:S(2)}) copy-start(s32[1,32]{1,0:T(1,128)} %param.20) | copy-start | bytes 388
  549.7 137.7 %all-gather.16.cloned.1.call-start = ((), (), s32[]{:S(2)}) async-start(), calls=%async_computation.14 | async-start | bytes 4055040 | tf_op jit(solution)/shard_map/all_gather | solution.py:35
  638.0 6.1 copy-start.4
  638.9 89.9 %all-gather.18.cloned.1.call-start = ((), (), s32[]{:S(2)}) async-start(), calls=%async_computation.15 | async-start | bytes 4096000 | tf_op jit(solution)/shard_map/all_gather | solution.py:190
  642.5 2.0 copy-start.11
  694.5 19.8 %all-to-all-start.2 = ((bf16[32,48,160]{2,1,0:T(8,128)(2,1)}), bf16[32,48,160]{2,1,0:T(8,128)(2,1)S(1)}, u32[]{:S(2)}, u32[]{:S(2)}) async-start(bf16[32,48,160]{2,1,0:T(8,128)(2,1)} %copy.123), calls=%async_computation.5 | async-start | bytes 1572864 | tf_op jit(solution)/shard_map/all_to_all | solution.py:39
Sparse Core Ops, SparseCore 0:
  10.8 49.2 all-gather.7
  80.6 43.5 all-gather.9
  157.0 100.1 all-reduce.1
  261.1 74.5 reduce-scatter.5
  339.9 89.5 reduce-scatter.3
  432.4 47.0 all-gather.11
  498.2 43.6 all-gather.13
  549.8 87.1 reduce-scatter.7
  639.9 47.5 all-gather.15
  688.9 39.8 all-gather.17
where the time goes:
time: 744 us; the launch traced here: 740 us
  waiting for transfers between devices  445 us (60%)
  local copies, waits for them, and re-layouts  135 us (18%)
  matrix products  56.5 us (8%)
  blocking collectives  54.9 us (7%)
  other arithmetic  25.4 us (3%)
  between operations  16.9 us (2%)
    all_gather x4, waiting for transfers between devices, row_blocks(): lax.all_gather(values, 'blk', axis=0, tiled=True)  142 us
    reduce_scatter x1, waiting for transfers between devices, on_device(): lax.psum_scatter(num_scaled, 'blk', scatter_dimension=0, tiled=True)  93.1 us
    reduce_scatter x1, waiting for transfers between devices, on_device(): lax.psum_scatter(jnp.dot(hidden_all, w_down, preferred_element_type=jnp.f...  87.3 us
    pmax x1, waiting for transfers between devices, on_device(): max_all = lax.pmax(request_max, 'blk')  86.9 us
    all_to_all x2, blocking collectives, column_blocks(): lax.all_to_all(values, 'blk', split_axis=0, concat_axis=1, tiled=True)  27.9 us
    all_gather x1, blocking collectives, on_device(): received = lax.all_gather(send_rows, 'blk', axis=0, tiled=True)  26.9 us
    reduce_scatter x1, waiting for transfers between devices, on_device(): lax.psum_scatter(den_scaled, 'blk', scatter_dimension=0, tiled=True)  26.3 us
    mul x1, local copies, waits for them, and re-layouts, on_device(): num_part.reshape(requests, tree_rows, H, HD) * factor[..., None]  16.4 us
  transfers between devices with their start and end apart: 11, of which 11 were waited for; matrix products, arithmetic and copies ran while one was open for 20% of the time, Pallas kernels for 0%

commit v1 on v0

--- a/solution.py
+++ b/solution.py
@@ -14,6 +14,13 @@
 LEVEL_START = (0, 1, 5, 15, 30, 48)
 
 
+def all_by_exchange(array, axis, dim):
+    size = lax.axis_size(axis)
+    blocks = jnp.stack([array for _ in range(size)])
+    blocks = lax.all_to_all(blocks, axis, split_axis=0, concat_axis=0)
+    return jnp.concatenate(blocks, axis=dim)
+
+
 def rms_rows(values):
     wide = values.astype(jnp.float32)
     return (wide * lax.rsqrt(jnp.mean(wide * wide, axis=-1, keepdims=True) + EPS)).astype(
@@ -32,7 +39,7 @@
 
 
 def row_blocks(values, mapper):
-    return mapper(lax.all_gather(values, "blk", axis=0, tiled=True), jnp.int32(0))
+    return mapper(all_by_exchange(values, "blk", 0), jnp.int32(0))
 
 
 def column_blocks(values):

time: 744 us -> 798 us (1.073)
  blocking collectives: 54.9 us -> 248 us
  waiting for transfers between devices: 445 us -> 298 us
    all_to_all x0 -> x3, blocking collectives: none -> 163 us  [all_by_exchange(): blocks = lax.all_to_all(blocks, axis, split_axis=0, concat_axis=0)]
    all_gather x4 -> x0, waiting for transfers between devices: 142 us -> none  [row_blocks(): lax.all_gather(values, 'blk', axis=0, tiled=True)]
    all_gather x1, blocking collectives: 26.9 us -> 59.5 us  [on_device(): received = lax.all_gather(send_rows, 'blk', axis=0, tiled=True)]
  transfers between devices with their start and end apart: 11 -> 8, of which waited for: 11 -> 6; matrix products, arithmetic and copies ran while one was open for 20% -> 19% of each run, Pallas kernels for 0% -> 0%
where the time goes in v1:
time: 798 us; the launch traced here: 793 us
  waiting for transfers between devices  298 us (37%)
  blocking collectives  248 us (31%)
  local copies, waits for them, and re-layouts  137 us (17%)
  matrix products  52.1 us (7%)
  other arithmetic  26.2 us (3%)
  between operations  18 us (2%)
  starting transfers between devices  14 us (2%)
    all_to_all x3, blocking collectives, all_by_exchange(): blocks = lax.all_to_all(blocks, axis, split_axis=0, concat_axis=0)  163 us
    reduce_scatter x1, waiting for transfers between devices, on_device(): lax.psum_scatter(num_scaled, 'blk', scatter_dimension=0, tiled=True)  93.1 us
    reduce_scatter x1, waiting for transfers between devices, on_device(): lax.psum_scatter(jnp.dot(hidden_all, w_down, preferred_element_type=jnp.f...  86.5 us
    pmax x1, waiting for transfers between devices, on_device(): max_all = lax.pmax(request_max, 'blk')  84.9 us
    all_gather x1, blocking collectives, on_device(): received = lax.all_gather(send_rows, 'blk', axis=0, tiled=True)  59.5 us
    reduce_scatter x1, waiting for transfers between devices, on_device(): lax.psum_scatter(den_scaled, 'blk', scatter_dimension=0, tiled=True)  26.5 us
    all_to_all x2, blocking collectives, column_blocks(): lax.all_to_all(values, 'blk', split_axis=0, concat_axis=1, tiled=True)  25.1 us
    mul x1, local copies, waits for them, and re-layouts, on_device(): num_part.reshape(requests, tree_rows, H, HD) * factor[..., None]  16.4 us
  transfers between devices with their start and end apart: 8, of which 6 were waited for; matrix products, arithmetic and copies ran while one was open for 19% of the time, Pallas kernels for 0%

profile of v1, /device:TPU:1, one launch (start us, length us, event | category | flops | bytes accessed | tf_op | source)
XLA Modules:
  0.0 792.8 jit_solution(12654976365805552666)
XLA Ops:
  10.4 56.3 %all_to_all.65 = bf16[32,48,1280]{2,1,0:T(8,128)(2,1)S(1)} all-to-all(bf16[32,48,1280]{2,1,0:T(8,128)(2,1)S(1)} %stack.14), channel_id=1, replica_groups=mesh['req'=4,'blk'=32] {'blk'}, dimensions={0} | all-to-all | bytes 7864320 | tf_op jit(solution)/shard_map/all_to_all | solution.py:20
  68.3 13.8 %all_to_all.66 = bf16[32,48,120]{2,1,0:T(8,128)(2,1)S(1)} all-to-all(bf16[32,48,120]{2,1,0:T(8,128)(2,1)S(1)} %bitcast.187), channel_id=1, replica_groups=mesh['req'=4,'blk'=32] {'blk'}, dimensions={0} | all-to-all | bytes 737280 | tf_op jit(solution)/shard_map/all_to_all | solution.py:46
  84.0 10.6 %slice_bitcast_fusion.1 = (bf16[2048,1280]{1,0:T(8,128)(2,1)}, bf16[2048,1280]{1,0:T(8,128)(2,1)}, bf16[1,1,2048,1280]{3,2,1,0:T(8,128)(2,1)}, bf16[1,1,2048,1280]{3,2,1,0:T(8,128)(2,1)}) fusion(bf16[1,2,2048,1280]{3,2,1,0:T(8,128)(2,1)} %param.16), kind=kLoop, calls=%fused_computation.218 | loop fusion | bytes 31457280 | tf_op jit(solution)/shard_map/squeeze | solution.py:222
  94.6 15.7 %reshape.1072 = bf16[16,128,16,80]{3,2,1,0:T(8,128)(2,1)} reshape(bf16[1,1,2048,1280]{3,2,1,0:T(8,128)(2,1)} %get-tuple-element.30) | data formatting | bytes 10485760 | tf_op jit(solution)/shard_map/reshape;squeeze | solution.py:103
  110.3 15.8 %reshape.1073 = bf16[16,128,16,80]{3,2,1,0:T(8,128)(2,1)} reshape(bf16[1,1,2048,1280]{3,2,1,0:T(8,128)(2,1)} %get-tuple-element.29) | data formatting | bytes 10485760 | tf_op jit(solution)/shard_map/reshape;squeeze | solution.py:104
  128.1 12.1 %reshape.918 = bf16[32,48,16,80]{3,2,1,0:T(8,128)(2,1)} reshape(bf16[1536,1280]{1,0:T(8,128)(2,1)} %all-gather.4.cloned.1.call-done) | data formatting | bytes 7864320 | tf_op jit(solution)/shard_map/reshape | solution.py:101
  140.1 5.4 gather_fusion
  147.8 10.6 %bitcast_reduce_fusion = (f32[16,48,16]{1,2,0:T(8,128)S(1)}, f32[16,16,48,128]{3,2,1,0:T(8,128)}) fusion(pred[16,128]{1,0:T(8,128)(4,1)S(1)} %add_compare_fusion, bf16[16,128,16,80]{3,2,1,0:T(8,128)(2,1)} %reshape.1072, bf16[16,48,16,80]{3,2,1,0:T(8,128)(2,1)S(1)} %broadcast_select_fusion), kind=kOutput, calls=%fused_computation.15 | convolution fusion | flops 256364544 | bytes 13551616 | tf_op jit(solution)/shard_map/pqhd,pthd->pqht/dot_general | solution.py:106
  161.2 9.3 %fusion.23 = f32[16,48,16,80]{3,1,2,0:T(8,128)} fusion(bf16[16,128,16,80]{3,2,1,0:T(8,128)(2,1)} %reshape.1073, f32[16,16,48,128]{3,2,1,0:T(8,128)} %get-tuple-element.38, f32[16,48,16]{1,2,0:T(8,128)S(1)} %broadcast_select_fusion.1, pred[16,128]{1,0:T(8,128)(4,1)S(1)} %add_compare_fusion), kind=kOutput, calls=%fused_computation.37 | convolution fusion | flops 259522560 | bytes 15517696 | tf_op jit(solution)/shard_map/pqht,pthd->pqhd/dot_general | solution.py:114
  170.5 5.7 fusion.8
  176.2 84.9 %all-reduce.2.cloned.1.call-done = f32[32,48,16]{1,0,2:T(8,128)} async-done(((f32[32,48,16]{1,0,2:T(8,128)}), f32[32,48,16]{1,0,2:T(8,128)}) %all-reduce.2.cloned.1.call-update) | async-done | bytes 98320 | tf_op jit(solution)/shard_map/pmax | solution.py:122
  263.7 13.1 %broadcast_multiply_fusion = f32[32,48,16,80]{3,0,2,1:T(8,128)} fusion(f32[32,48,16]{0,2,1:T(8,128)S(1)} %copy.110, f32[16,48,16,80]{3,1,2,0:T(8,128)} %fusion.23, s32[16]{0:T(128)S(1)} %convert_reduce_fusion), kind=kOutput, calls=%fused_computation.20 | convolution fusion | flops 379453952 | bytes 11894848 | tf_op jit(solution)/shard_map/pr,pqhd->rqhd/dot_general | solution.py:119
  276.9 16.4 %copy.111 = f32[32,48,16,80]{3,2,1,0:T(8,128)} copy(f32[32,48,16,80]{3,0,2,1:T(8,128)} %broadcast_multiply_fusion) | data formatting | bytes 15728640 | tf_op jit(solution)/shard_map/mul | solution.py:125
  293.3 12.8 %reshape.919 = f32[32,48,1280]{2,1,0:T(8,128)} reshape(f32[32,48,16,80]{3,2,1,0:T(8,128)} %copy.111) | data formatting | bytes 15728640 | tf_op jit(solution)/shard_map/reshape | solution.py:125
  313.2 26.5 %reduce-scatter.6.cloned.1.call-done = f32[1,48,16]{1,2,0:T(8,128)} async-done(((f32[32,48,16]{1,2,0:T(8,128)}), f32[1,48,16]{1,2,0:T(8,128)}) %reduce-scatter.6.cloned.1.call-update) | async-done | bytes 3088 | tf_op jit(solution)/shard_map/reduce_scatter | solution.py:129
  340.4 93.1 %reduce-scatter.4.cloned.1.call-done = f32[1,48,1280]{2,1,0:T(8,128)} async-done(((f32[32,48,1280]{2,1,0:T(8,128)}), f32[1,48,1280]{2,1,0:T(8,128)}) %reduce-scatter.4.cloned.1.call-update) | async-done | bytes 245776 | tf_op jit(solution)/shard_map/reduce_scatter | solution.py:130
  435.6 55.1 %all_to_all.67 = bf16[32,48,1280]{2,1,0:T(8,128)(2,1)S(1)} all-to-all(bf16[32,48,1280]{2,1,0:T(8,128)(2,1)S(1)} %stack.15), channel_id=1, replica_groups=mesh['req'=4,'blk'=32] {'blk'}, dimensions={0} | all-to-all | bytes 7864320 | tf_op jit(solution)/shard_map/all_to_all | solution.py:20
  492.9 11.3 %all_to_all.68 = bf16[32,2,960]{2,1,0:T(2,128)(2,1)S(1)} all-to-all(bf16[32,2,960]{2,1,0:T(2,128)(2,1)S(1)} %reshape.1081), channel_id=1, replica_groups=mesh['req'=4,'blk'=32] {'blk'}, dimensions={0} | all-to-all | bytes 245760 | tf_op jit(solution)/shard_map/all_to_all | solution.py:46
  505.4 51.8 %all_to_all.69 = bf16[32,48,1280]{2,1,0:T(8,128)(2,1)} all-to-all(bf16[32,48,1280]{2,1,0:T(8,128)(2,1)S(1)} %stack.16), channel_id=1, replica_groups=mesh['req'=4,'blk'=32] {'blk'}, dimensions={0} | all-to-all | bytes 7864320 | tf_op jit(solution)/shard_map/all_to_all | solution.py:20
  557.2 7.8 fusion.66
  565.0 86.5 %reduce-scatter.8.cloned.1.call-done = f32[48,1280]{1,0:T(8,128)} async-done(((f32[1536,1280]{1,0:T(8,128)}), f32[48,1280]{1,0:T(8,128)}) %reduce-scatter.8.cloned.1.call-update) | async-done | bytes 245776 | tf_op jit(solution)/shard_map/reduce_scatter | solution.py:169
  655.7 7.5 all-to-all-start.5
  669.6 59.5 %all-gather = bf16[32,5,2560]{2,1,0:T(8,128)(2,1)S(1)} all-gather(bf16[1,5,2560]{2,1,0:T(8,128)(2,1)S(1)} %fusion.12), channel_id=1, replica_groups=mesh['req'=4,'blk'=32] {'blk'}, dimensions={0}, use_global_device_ids=true | all-gather | bytes 844800 | tf_op jit(solution)/shard_map/all_gather | solution.py:208
  729.4 7.1 scatter_custom_fusion
  736.6 7.2 scatter_custom_fusion.1
  743.8 3.5 fusion.119
  750.9 5.4 all-to-all-start.6
  756.3 9.1 %maximum_bitcast_fusion = bf16[1,2,2048,1280]{3,2,1,0:T(8,128)(2,1)} fusion(bf16[1,2048,1280]{2,1,0:T(8,128)(2,1)} %bitcast.180, bf16[1,2048,1280]{2,1,0:T(8,128)(2,1)} %bitcast.181), kind=kLoop, calls=%fused_computation.9 | loop fusion | flops 5242880 | bytes 20971520 | tf_op jit(solution)/shard_map/broadcast_in_dim | solution.py:224
  765.4 5.1 all-to-all-done.6
  772.8 3.0 reshape.957
  778.0 3.3 reshape.949
  781.3 4.1 fusion.28
  (148 shorter events, 45.3 us)
Async XLA Ops:
  8.0 735.8 %copy-start = (bf16[4,1280,40]{1,2,0:T(8,128)(2,1)S(1)}, bf16[4,1280,40]{1,2,0:T(8,128)(2,1)}, u32[]{:S(2)}) copy-start(bf16[4,1280,40]{1,2,0:T(8,128)(2,1)} %param.25) | copy-start | bytes 1228804
  8.0 120.1 %all-gather.4.cloned.1.call-start = ((), (), s32[]{:S(2)}) async-start(), calls=%async_computation.10 | async-start | bytes 4055040 | tf_op jit(solution)/shard_map/all_gather | solution.py:79
  10.1 56.6 %copy-start.9 = (bf16[1280,120]{0,1:T(8,128)(2,1)S(1)}, bf16[1280,120]{0,1:T(8,128)(2,1)}, u32[]{:S(2)}) copy-start(bf16[1280,120]{0,1:T(8,128)(2,1)} %param.21) | copy-start | bytes 921604
  66.7 17.0 %copy-start.8 = (s32[1,32]{1,0:T(1,128)S(1)}, s32[1,32]{1,0:T(1,128)}, u32[]{:S(2)}) copy-start(s32[1,32]{1,0:T(1,128)} %param.18) | copy-start | bytes 388
  83.5 177.6 %all-reduce.2.cloned.1.call-start = ((), (), s32[]{:S(2)}) async-start(), calls=%async_computation.11 | async-start | bytes 524288 | tf_op jit(solution)/shard_map/pmax | solution.py:122
  110.3 15.8 %copy-start.1 = (s32[1,512]{1,0:T(1,128)S(1)}, s32[1,512]{1,0:T(1,128)}, u32[]{:S(2)}) copy-start(s32[1,512]{1,0:T(1,128)} %param.17) | copy-start | bytes 6148
  160.8 178.9 %reduce-scatter.6.cloned.1.call-start = ((), (), s32[]{:S(2)}) async-start(), calls=%async_computation.13 | async-start | bytes 270336 | tf_op jit(solution)/shard_map/reduce_scatter | solution.py:129
  263.7 169.8 %reduce-scatter.4.cloned.1.call-start = ((), (), s32[]{:S(2)}) async-start(), calls=%async_computation.12 | async-start | bytes 8110080 | tf_op jit(solution)/shard_map/reduce_scatter | solution.py:130
  306.1 0.7 copy-start.2
  306.1 345.5 %reduce-scatter.8.cloned.1.call-start = ((), (), s32[]{:S(2)}) async-start(), calls=%async_computation.14 | async-start | bytes 8110080 | tf_op jit(solution)/shard_map/reduce_scatter | solution.py:169
  435.4 55.4 %copy-start.5 = (bf16[1280,40]{0,1:T(8,128)(2,1)S(1)}, bf16[1280,40]{0,1:T(8,128)(2,1)}, u32[]{:S(2)}) copy-start(bf16[1280,40]{0,1:T(8,128)(2,1)} %param.22) | copy-start | bytes 307204
  490.7 14.2 %copy-start.3 = (bf16[48,1280]{1,0:T(8,128)(2,1)S(1)}, bf16[48,1280]{1,0:T(8,128)(2,1)}, u32[]{:S(2)}) copy-start(bf16[48,1280]{1,0:T(8,128)(2,1)} %param.15) | copy-start | bytes 368644
  505.2 52.1 %copy-start.6 = (bf16[40,1280]{1,0:T(8,128)(2,1)S(1)}, bf16[40,1280]{1,0:T(8,128)(2,1)}, u32[]{:S(2)}) copy-start(bf16[40,1280]{1,0:T(8,128)(2,1)} %param.24) | copy-start | bytes 307204
  505.2 52.1 %copy-start.7 = (bf16[1280,40]{0,1:T(8,128)(2,1)S(1)}, bf16[1280,40]{0,1:T(8,128)(2,1)}, u32[]{:S(2)}) copy-start(bf16[1280,40]{0,1:T(8,128)(2,1)} %param.23) | copy-start | bytes 307204
  653.3 2.4 copy-start.4
  655.7 8.1 %copy-start.10 = (s32[1,32]{1,0:T(1,128)S(1)}, s32[1,32]{1,0:T(1,128)}, u32[]{:S(2)}) copy-start(s32[1,32]{1,0:T(1,128)} %param.20) | copy-start | bytes 388
  655.7 88.1 %all-to-all-start.5 = ((bf16[32,48,1280]{2,1,0:T(8,128)(2,1)}), bf16[32,48,1280]{2,1,0:T(8,128)(2,1)}, u32[]{:S(2)}, u32[]{:S(2)}) async-start(bf16[32,48,1280]{2,1,0:T(8,128)(2,1)} %stack.17), calls=%async_computation.8 | async-start | bytes 7864320 | tf_op jit(solution)/shard_map/all_to_all | solution.py:20
  663.2 118.1 %all-gather.6.cloned.1.call-start = ((), (), s32[]{:S(2)}) async-start(), calls=%async_computation.15 | async-start | bytes 4096000 | tf_op jit(solution)/shard_map/all_gather | solution.py:197
  666.8 2.0 copy-start.11
  750.9 19.7 %all-to-all-start.6 = ((bf16[32,48,160]{2,1,0:T(8,128)(2,1)}), bf16[32,48,160]{2,1,0:T(8,128)(2,1)S(1)}, u32[]{:S(2)}, u32[]{:S(2)}) async-start(bf16[32,48,160]{2,1,0:T(8,128)(2,1)} %copy.123), calls=%async_computation.9 | async-start | bytes 1572864 | tf_op jit(solution)/shard_map/all_to_all | solution.py:46
Sparse Core Ops, SparseCore 0:
  83.6 44.4 all-gather.3
  160.9 100.1 all-reduce.1
  265.1 74.5 reduce-scatter.5
  343.9 89.5 reduce-scatter.3
  565.2 86.3 reduce-scatter.7
Sparse Core Ops, SparseCore 1:
  665.4 41.7 all-gather.5
